TPU v7x, 32 devices: a whole 2x2x4 slice. The times are simulated.
32 devices in a mesh: groups: 2 (over y), roll: 4 (over z), tp: 2 (over x), seq: 2 (over core).
Axes of the slice: x: 2, y: 2, z: 4, core: 2. Of those that a mesh axis runs over, the one named last changes fastest.
Arguments:
- hidden: bfloat16 [128, 8192], P('groups', ('roll', 'seq')), parts along dimension 0, may hold values from -6 to 6
- w_query: bfloat16 [8192, 8192], P(('roll', 'seq'), 'tp'), may hold values from -0.0625 to 0.0625
- w_key: bfloat16 [8192, 1024], P(('roll', 'seq'), 'tp'), may hold values from -0.0625 to 0.0625
- w_value: bfloat16 [8192, 1024], P(('roll', 'seq'), 'tp'), may hold values from -0.0625 to 0.0625
- b_query: bfloat16 [8192], P('tp'), may hold values from -12 to 12
- b_key: bfloat16 [1024], P('tp'), may hold values from -12 to 12
- b_value: bfloat16 [1024], P('tp'), may hold values from -6 to 6
- w_out: bfloat16 [8192, 8192], P('tp', ('roll', 'seq')), may hold values from -0.0625 to 0.0625
- prefix_keys: bfloat16 [4, 4096, 1024], P('groups', ('roll', 'seq'), 'tp'), parts along dimension 0, may hold values from -256 to 256
- prefix_values: bfloat16 [4, 4096, 1024], P('groups', ('roll', 'seq'), 'tp'), parts along dimension 0, may hold values from -6 to 6
- suffix_keys: bfloat16 [16, 2048, 1024], P(('groups', 'roll'), 'seq', 'tp'), parts along dimension 0, may hold values from -6 to 6
- suffix_values: bfloat16 [16, 2048, 1024], P(('groups', 'roll'), 'seq', 'tp'), parts along dimension 0, may hold values from -6 to 6
- suffix_lengths: int32 [16], P('groups'), parts along dimension 0, may hold values from 1 to 2048, 8192 in all
- prompt_of: int32 [16], P('groups'), parts along dimension 0, may hold values from 0 to 1, as said below
Outputs:
- attended: bfloat16 [128, 8192], P(('groups', 'tp'), ('roll', 'seq')), parts along dimension 0
There are 2 independent parts, one for each index of `groups`. A program takes and returns all parts, laid end to end along the dimension named above; an argument that names none is the same for every part. Nothing has to cross between parts.
Inputs may be any that keep to these rules, and one draw needn't show every extreme that they name: Only the first suffix_lengths[r] rows of a rollout's suffix cache are live; the lengths of a group add up to 8192 and the largest is exactly 2048. `prompt_of`: every prompt is extended by exactly 4 rollouts.
All inputs are finite; a program needn't handle non-finite values.
Results may differ from a plain program's by a relative error of at most 0.009.
The roundings to bfloat16 on the way count: a program that leaves them out, or rounds other values in their place, can miss the bound.
Values may be sent and summed in bfloat16 or wider, within the bound.
No kernel may reach another device: no remote copies, remote signals or barrier semaphores. Data moves between devices by JAX's collectives and lax.ppermute only.
A program may use at most 128 MiB of HBM per device.

v0:
```python
import math
import jax
import jax.numpy as jnp
from jax import lax
from jax.sharding import PartitionSpec as P

HD = 128
GUESS = 8
ROPE_BASE = 1000000.0
NEG_FILL = -1e30


def rotate(values, positions):
    half = values.shape[-1] // 2
    steps = jnp.arange(half).astype(jnp.float32) * (2.0 / values.shape[-1])
    freqs = jnp.exp(-math.log(ROPE_BASE) * steps)
    angles = positions[:, None] * freqs[None, :]
    cosine = jnp.cos(angles)[:, None, :]
    sine = jnp.sin(angles)[:, None, :]
    first = values[..., :half]
    second = values[..., half:]
    return jnp.concatenate(
        [first * cosine - second * sine, second * cosine + first * sine], axis=-1
    )


def lookup(table, indices):
    hits = indices[:, None] == jnp.arange(table.shape[0], dtype=jnp.int32)[None, :]
    return jnp.sum(jnp.where(hits, table[None, :], 0), axis=1)


def combine(first, second):
    peak_a, total_a, numer_a = first
    peak_b, total_b, numer_b = second
    peak = jnp.maximum(peak_a, peak_b)
    factor_a = jnp.exp(peak_a - peak)
    factor_b = jnp.exp(peak_b - peak)
    return (
        peak,
        total_a * factor_a + total_b * factor_b,
        numer_a * factor_a[..., None] + numer_b * factor_b[..., None],
    )


def masked_stats(scores, visible, values):
    peak = jnp.max(jnp.where(visible, scores, NEG_FILL), axis=-1)
    weights = jnp.exp(jnp.where(visible, scores - peak[..., None], NEG_FILL))
    total = jnp.sum(weights, axis=-1)
    numer = jnp.einsum(
        "rtkgs,rskd->rtkgd",
        weights.astype(jnp.bfloat16),
        values,
        preferred_element_type=jnp.float32,
    )
    return (peak, total, numer)


def body(
    hidden,
    w_query,
    w_key,
    w_value,
    b_query,
    b_key,
    b_value,
    w_out,
    prefix_keys,
    prefix_values,
    suffix_keys,
    suffix_values,
    suffix_lengths,
    prompt_of,
):
    row_count = hidden.shape[0]
    q_heads = w_query.shape[1] // HD
    kv_heads = w_key.shape[1] // HD
    group = q_heads // kv_heads
    prompts = prefix_keys.shape[0]
    pre_dev = prefix_keys.shape[1]
    prefix_total = pre_dev * lax.axis_size(("roll", "seq"))
    per_device = suffix_keys.shape[0]
    suf_dev = suffix_keys.shape[1]
    scale = 1.0 / math.sqrt(HD)
    q_part = jnp.dot(hidden, w_query, preferred_element_type=jnp.float32)
    k_part = jnp.dot(hidden, w_key, preferred_element_type=jnp.float32)
    v_part = jnp.dot(hidden, w_value, preferred_element_type=jnp.float32)
    q_sum, k_sum, v_sum = lax.psum((q_part, k_part, v_part), ("roll", "seq"))
    count = q_sum.shape[0]
    row_ids = jnp.arange(count, dtype=jnp.int32)
    owner_ids = row_ids // GUESS
    positions = (prefix_total + lookup(suffix_lengths, owner_ids) + row_ids % GUESS).astype(
        jnp.float32
    )
    q_rot = rotate((q_sum + b_query.astype(jnp.float32)).reshape(count, q_heads, HD), positions)
    k_rot = rotate((k_sum + b_key.astype(jnp.float32)).reshape(count, kv_heads, HD), positions)
    v_fin = (v_sum + b_value.astype(jnp.float32)).reshape(count, kv_heads, HD)
    query = q_rot.astype(jnp.bfloat16)
    key_new = k_rot.astype(jnp.bfloat16)
    value_new = v_fin.astype(jnp.bfloat16)
    query_grid = query.reshape(row_count, kv_heads, group, HD)
    owners_all = jnp.arange(row_count, dtype=jnp.int32) // GUESS
    row_prompt = lookup(prompt_of, owners_all)
    pre_keys = prefix_keys.reshape(prompts, pre_dev, kv_heads, HD)
    pre_values = prefix_values.reshape(prompts, pre_dev, kv_heads, HD)
    peak_all = jnp.full((row_count, kv_heads, group), NEG_FILL, jnp.float32)
    total_all = jnp.zeros((row_count, kv_heads, group), jnp.float32)
    numer_all = jnp.zeros((row_count, kv_heads, group, HD), jnp.float32)
    for prompt in range(prompts):
        scores = (
            jnp.einsum(
                "tkgd,skd->tkgs", query_grid, pre_keys[prompt], preferred_element_type=jnp.float32
            )
            * scale
        )
        block_peak = jnp.max(scores, axis=-1)
        weights = jnp.exp(scores - block_peak[..., None])
        block_numer = jnp.einsum(
            "tkgs,skd->tkgd",
            weights.astype(jnp.bfloat16),
            pre_values[prompt],
            preferred_element_type=jnp.float32,
        )
        picked = (row_prompt == prompt)[:, None, None]
        peak_all = jnp.where(picked, block_peak, peak_all)
        total_all = jnp.where(picked, jnp.sum(weights, axis=-1), total_all)
        numer_all = jnp.where(picked[..., None], block_numer, numer_all)
    first_rollout = lax.axis_index("roll") * per_device
    seq_index = lax.axis_index("seq")
    local_len = lax.dynamic_slice_in_dim(suffix_lengths, first_rollout, per_device, 0)
    live = jnp.clip(local_len - seq_index * suf_dev, 0, suf_dev)
    row_start = first_rollout * GUESS
    local_rows = per_device * GUESS
    query_local = lax.dynamic_slice_in_dim(query_grid, row_start, local_rows, 0).reshape(
        per_device, GUESS, kv_heads, group, HD
    )
    suf_keys = suffix_keys.reshape(per_device, suf_dev, kv_heads, HD)
    suf_values = suffix_values.reshape(per_device, suf_dev, kv_heads, HD)
    scores = (
        jnp.einsum("rtkgd,rskd->rtkgs", query_local, suf_keys, preferred_element_type=jnp.float32)
        * scale
    )
    visible = (jnp.arange(suf_dev, dtype=jnp.int32)[None, :] < live[:, None])[
        :, None, None, None, :
    ]
    suffix_part = masked_stats(scores, visible, suf_values)
    key_local = lax.dynamic_slice_in_dim(key_new, row_start, local_rows, 0).reshape(
        per_device, GUESS, kv_heads, HD
    )
    value_local = lax.dynamic_slice_in_dim(value_new, row_start, local_rows, 0).reshape(
        per_device, GUESS, kv_heads, HD
    )
    new_scores = (
        jnp.einsum("rtkgd,rskd->rtkgs", query_local, key_local, preferred_element_type=jnp.float32)
        * scale
    )
    guess_ids = jnp.arange(GUESS, dtype=jnp.int32)
    causal = (guess_ids[None, :] <= guess_ids[:, None]) & (seq_index == 0)
    guess_part = masked_stats(new_scores, causal[None, :, None, None, :], value_local)
    prefix_local = (
        lax.dynamic_slice_in_dim(peak_all, row_start, local_rows, 0).reshape(
            per_device, GUESS, kv_heads, group
        ),
        lax.dynamic_slice_in_dim(total_all, row_start, local_rows, 0).reshape(
            per_device, GUESS, kv_heads, group
        ),
        lax.dynamic_slice_in_dim(numer_all, row_start, local_rows, 0).reshape(
            per_device, GUESS, kv_heads, group, HD
        ),
    )
    peak_loc, total_loc, numer_loc = combine(combine(prefix_local, suffix_part), guess_part)
    peak_all = lax.dynamic_update_slice_in_dim(
        peak_all, peak_loc.reshape(local_rows, kv_heads, group), row_start, 0
    )
    total_all = lax.dynamic_update_slice_in_dim(
        total_all, total_loc.reshape(local_rows, kv_heads, group), row_start, 0
    )
    numer_all = lax.dynamic_update_slice_in_dim(
        numer_all, numer_loc.reshape(local_rows, kv_heads, group, HD), row_start, 0
    )
    peaks, totals, numers = (
        lax.all_to_all(peak_all[None], ("roll", "seq"), split_axis=1, concat_axis=0, tiled=True),
        lax.all_to_all(total_all[None], ("roll", "seq"), split_axis=1, concat_axis=0, tiled=True),
        lax.all_to_all(numer_all[None], ("roll", "seq"), split_axis=1, concat_axis=0, tiled=True),
    )
    peak_top = jnp.max(peaks, axis=0)
    factors = jnp.exp(peaks - peak_top[None])
    share = (
        jnp.sum(numers * factors[..., None], axis=0) / jnp.sum(totals * factors, axis=0)[..., None]
    )
    share = share.astype(jnp.bfloat16).reshape(share.shape[0], q_heads * HD)
    attention = lax.all_gather(share, ("roll", "seq"), axis=0, tiled=True)
    summed = lax.psum_scatter(
        jnp.dot(attention, w_out, preferred_element_type=jnp.float32),
        "tp",
        scatter_dimension=0,
        tiled=True,
    )
    return summed.astype(jnp.bfloat16)


def solution(mesh):
    return jax.shard_map(
        body,
        mesh=mesh,
        in_specs=(
            P("groups", ("roll", "seq")),
            P(("roll", "seq"), "tp"),
            P(("roll", "seq"), "tp"),
            P(("roll", "seq"), "tp"),
            P("tp"),
            P("tp"),
            P("tp"),
            P("tp", ("roll", "seq")),
            P("groups", ("roll", "seq"), "tp"),
            P("groups", ("roll", "seq"), "tp"),
            P(("groups", "roll"), "seq", "tp"),
            P(("groups", "roll"), "seq", "tp"),
            P("groups"),
            P("groups"),
        ),
        out_specs=P(("groups", "tp"), ("roll", "seq")),
        check_vma=False,
    )
```

profile of v0, /device:TPU:0, one launch (start us, length us, event | category | flops | bytes accessed | tf_op | source)
XLA Modules:
  0.0 188.1 jit_solution(5365839674309538938)
XLA Ops:
  6.6 6.2 %fusion.91 = f32[64,4096]{1,0:T(8,128)} fusion(bf16[64,1024]{1,0:T(8,128)(2,1)} %param.14, bf16[1024,4096]{1,0:T(8,128)(2,1)} %param.15), kind=kOutput, calls=%fused_computation.143 | convolution fusion | flops 536870912 | bytes 9568256 | tf_op jit(solution)/shard_map/dot_general | solution.py:84
  12.8 1.0 fusion.92
  13.8 0.9 fusion.93
  15.5 4.0 %reshape.290 = bf16[2,1024,4,128]{3,2,1,0:T(4,128)(2,1)} reshape(bf16[2,1024,512]{2,1,0:T(8,128)(2,1)} %param.24) | data formatting | bytes 4194304 | tf_op jit(solution)/shard_map/reshape | solution.py:136
  19.5 0.6 dynamic-slice.4
  20.2 0.6 dynamic-slice.5
  20.8 1.3 fusion.89
  22.0 1.0 copy.245
  23.1 1.0 copy.243
  24.1 4.0 %reshape.291 = bf16[2,1024,4,128]{3,2,1,0:T(4,128)(2,1)} reshape(bf16[2,1024,512]{2,1,0:T(8,128)(2,1)} %param.25) | data formatting | bytes 4194304 | tf_op jit(solution)/shard_map/reshape | solution.py:137
  28.5 49.9 %all-reduce.3.cloned.1.call-done = (f32[64,4096]{1,0:T(8,128)}, f32[64,512]{1,0:T(8,128)}, f32[64,512]{1,0:T(8,128)}) async-done(((f32[64,4096]{1,0:T(8,128)}, f32[64,512]{1,0:T(8,128)}, f32[64,512]{1,0:T(8,128)}), (f32[64,4096]{1,0:T(8,128)}, f32[64,512]{1,0:T(8,128)}, f32[64,512]{1,0:T(8,128)})) %all-reduce.3.cloned.1.call-update) | async-done | bytes 1310736 | tf_op jit(solution)/shard_map/psum | solution.py:87
  78.4 1.3 add_bitcast_fusion
  80.2 0.5 fusion.50
  80.8 0.9 bitcast_reduce_fusion.1
  81.6 0.9 bitcast_reduce_fusion
  82.6 0.7 select_reduce_fusion
  83.5 1.1 copy-done.6
  84.6 2.3 %fusion.2 = (f32[64,4,8]{2,0,1:T(8,128)S(1)}, f32[64,4,8]{2,0,1:T(8,128)S(1)}) fusion(f32[4,64,8,512]{3,2,1,0:T(8,128)S(1)} %get-tuple-element.37, f32[64,4,8]{2,0,1:T(8,128)S(1)} %get-tuple-element.36, f32[64,4,8]{2,0,1:T(8,128)S(1)} %get-tuple-element.34, f32[4,64,8,512]{3,2,1,0:T(8,128)S(1)} %get-tuple-element.35), kind=kLoop, calls=%fused_computation.6 | loop fusion | flops 6287360 | bytes 8421376 | tf_op jit(solution)/shard_map/reduce_sum | solution.py:125
  87.1 0.9 fusion.12
  88.0 0.6 fusion.21
  88.8 0.7 fusion.63
  89.5 0.7 copy.324
  90.2 1.7 reshape.303
  91.9 3.5 %all-to-all-start.1 = ((f32[8,1,256]{2,1,0:T(1,128)}), f32[8,1,256]{2,1,0:T(1,128)S(1)}, u32[]{:S(2)}, u32[]{:S(2)}) async-start(f32[8,1,256]{2,1,0:T(1,128)} %reshape.303), calls=%async_computation.1 | async-start | bytes 16384 | tf_op jit(solution)/shard_map/all_to_all | solution.py:181
  95.3 3.2 %fusion.26 = f32[4,64,8,128]{3,2,1,0:T(8,128)S(1)} fusion(bf16[512,4,128,1]{0,2,3,1:T(8,128)(2,1)} %bitcast.189, f32[4,64,8,512]{3,2,1,0:T(8,128)} %copy-done.3, f32[64,4,8]{2,0,1:T(8,128)S(1)} %get-tuple-element.34, pred[64]{0:T(512)(128)(4,1)} %copy-done.20), kind=kOutput, calls=%fused_computation.28 | convolution fusion | flops 271843328 | bytes 5775424 | tf_op jit(solution)/shard_map/tkgs,skd->tkgd/dot_general | solution.py:117
  98.5 0.4 copy-done.2
  99.1 1.6 fusion.23
  100.6 1.0 copy-done.5
  101.6 0.7 constant_dynamic-slice_fusion.2
  102.3 0.6 convert_element_type.64
  103.0 0.8 constant_dynamic-slice_fusion
  103.7 2.6 %fusion.41 = f32[2,8,4,8,128]{4,3,1,2,0:T(8,128)S(1)} fusion(bf16[2,1024,4,128,1]{3,2,1,0,4:T(4,128)(2,1)} %bitcast.192, f32[2,4,8,8,1024]{4,3,2,1,0:T(8,128)S(1)} %get-tuple-element.39, f32[2,8,4,8]{3,1,2,0:T(8,128)S(1)} %get-tuple-element.38, pred[2,1024]{1,0:T(4,128)(4,1)S(1)} %iota_compare_fusion, f32[2,8,4,8,128]{4,3,1,0,2:T(8,128)} %bitcast.202, ...), kind=kOutput, calls=%fused_computation.37 | convolution fusion | flops 136577024 | bytes 4728832 | tf_op jit(solution)/shard_map/rtkgs,rskd->rtkgd/dot_general | solution.py:49
  106.3 0.3 fusion.34
  106.8 0.8 reshape.305
  107.6 4.9 %all-to-all-start.2 = ((f32[8,1,256]{2,1,0:T(1,128)}), f32[8,1,256]{2,1,0:T(1,128)S(1)}, u32[]{:S(2)}, u32[]{:S(2)}) async-start(f32[8,1,256]{2,1,0:T(1,128)} %reshape.305), calls=%async_computation.2 | async-start | bytes 16384 | tf_op jit(solution)/shard_map/all_to_all | solution.py:182
  112.4 0.7 constant_dynamic-update-slice_fusion
  113.1 2.4 %copy.197 = f32[1,64,4,8,128]{4,3,2,0,1:T(8,128)} copy(f32[1,64,4,8,128]{4,3,1,2,0:T(8,128)} %constant_dynamic-update-slice_fusion) | data formatting | bytes 2097152 | tf_op jit(solution)/shard_map/dynamic_update_slice | solution.py:177
  115.5 2.5 %all-to-all-done.2 = f32[8,1,256]{2,1,0:T(1,128)S(1)} async-done(((f32[8,1,256]{2,1,0:T(1,128)}), f32[8,1,256]{2,1,0:T(1,128)S(1)}, u32[]{:S(2)}, u32[]{:S(2)}) %all-to-all-start.2) | async-done | bytes 8224 | tf_op jit(solution)/shard_map/all_to_all | solution.py:182
  118.0 3.6 %all-to-all-start = ((f32[1,64,4,8,128]{4,3,2,0,1:T(8,128)}), f32[1,64,4,8,128]{4,3,2,0,1:T(8,128)S(1)}, u32[]{:S(2)}, u32[]{:S(2)}) async-start(f32[1,64,4,8,128]{4,3,2,0,1:T(8,128)} %copy.197), calls=%async_computation | async-start | bytes 2097152 | tf_op jit(solution)/shard_map/all_to_all | solution.py:183
  121.7 0.5 broadcast.227
  122.2 0.7 reduce.1
  123.3 0.7 reduce
  124.5 23.6 %all-to-all-done = f32[1,64,4,8,128]{4,3,2,0,1:T(8,128)S(1)} async-done(((f32[1,64,4,8,128]{4,3,2,0,1:T(8,128)}), f32[1,64,4,8,128]{4,3,2,0,1:T(8,128)S(1)}, u32[]{:S(2)}, u32[]{:S(2)}) %all-to-all-start) | async-done | bytes 1048608 | tf_op jit(solution)/shard_map/all_to_all | solution.py:183
  148.1 0.3 fusion.45
  148.6 14.9 %all_gather.3 = bf16[64,4096]{1,0:T(8,128)(2,1)S(1)} all-gather(bf16[8,4096]{1,0:T(8,128)(2,1)S(1)} %bitcast.203), channel_id=1, replica_groups=mesh['groups'=2,'roll'=4,'tp'=2,'seq'=2] {'roll','seq'}, dimensions={0}, use_global_device_ids=true | all-gather | bytes 589824 | tf_op jit(solution)/shard_map/all_gather | solution.py:191
  163.5 5.7 %fusion.94 = f32[64,1024]{1,0:T(8,128)} fusion(bf16[64,4096]{1,0:T(8,128)(2,1)S(1)} %all_gather.3, bf16[4096,1024]{1,0:T(8,128)(2,1)} %param.21), kind=kOutput, calls=%fused_computation.146 | convolution fusion | flops 536870912 | bytes 9175040 | tf_op jit(solution)/shard_map/dot_general | solution.py:193
  169.2 10.6 %reduce-scatter.2.cloned.1.call-done = f32[32,1024]{1,0:T(8,128)} async-done(((f32[64,1024]{1,0:T(8,128)}), f32[32,1024]{1,0:T(8,128)}) %reduce-scatter.2.cloned.1.call-update) | async-done | bytes 131088 | tf_op jit(solution)/shard_map/reduce_scatter | solution.py:192
  179.7 1.5 convert_element_type.68
  (96 shorter events, 3.5 us)
Async XLA Ops:
  6.5 6.3 %copy-start = (bf16[1024,512]{1,0:T(8,128)(2,1)S(1)}, bf16[1024,512]{1,0:T(8,128)(2,1)}, u32[]{:S(2)}) copy-start(bf16[1024,512]{1,0:T(8,128)(2,1)} %param.16) | copy-start | bytes 3145732
  6.5 6.3 %copy-start.9 = (bf16[64,1024]{1,0:T(8,128)(2,1)S(1)}, bf16[64,1024]{1,0:T(8,128)(2,1)}, u32[]{:S(2)}) copy-start(bf16[64,1024]{1,0:T(8,128)(2,1)} %param.14) | copy-start | bytes 393220
  6.5 7.2 %copy-start.10 = (bf16[1024,512]{1,0:T(8,128)(2,1)S(1)}, bf16[1024,512]{1,0:T(8,128)(2,1)}, u32[]{:S(2)}) copy-start(bf16[1024,512]{1,0:T(8,128)(2,1)} %param.17) | copy-start | bytes 3145732
  6.5 8.2 %copy-start.17 = (bf16[4096]{0:T(1024)(128)(2,1)S(1)}, bf16[4096]{0:T(1024)(128)(2,1)}, u32[]{:S(2)}) copy-start(bf16[4096]{0:T(1024)(128)(2,1)} %param.18) | copy-start | bytes 24580
  6.5 8.3 %copy-start.23 = (bf16[512]{0:T(512)(128)(2,1)S(1)}, bf16[512]{0:T(512)(128)(2,1)}, u32[]{:S(2)}) copy-start(bf16[512]{0:T(512)(128)(2,1)} %param.19) | copy-start | bytes 3076
  6.5 8.3 %copy-start.24 = (bf16[512]{0:T(512)(128)(2,1)S(1)}, bf16[512]{0:T(512)(128)(2,1)}, u32[]{:S(2)}) copy-start(bf16[512]{0:T(512)(128)(2,1)} %param.20) | copy-start | bytes 3076
  6.6 71.8 %all-reduce.3.cloned.1.call-start = ((), (), s32[]{:S(2)}) async-start(), calls=%async_computation.5 | async-start | bytes 2621440 | tf_op jit(solution)/shard_map/psum | solution.py:87
  12.8 2.1 %copy-start.11 = (bf16[2,512,512]{2,1,0:T(8,128)(2,1)S(1)}, bf16[2,512,512]{2,1,0:T(8,128)(2,1)}, u32[]{:S(2)}) copy-start(bf16[2,512,512]{2,1,0:T(8,128)(2,1)} %param.22) | copy-start | bytes 3145732
  12.8 2.6 %copy-start.22 = (s32[8]{0:T(128)S(1)}, s32[8]{0:T(128)}, u32[]{:S(2)}) copy-start(s32[8]{0:T(128)} %param.26) | copy-start | bytes 100
  12.8 2.6 %copy-start.27 = (s32[8]{0:T(128)S(1)}, s32[8]{0:T(128)}, u32[]{:S(2)}) copy-start(s32[8]{0:T(128)} %param.27) | copy-start | bytes 100
  15.5 8.6 %copy-start.18 = (pred[64]{0:T(512)(128)(4,1)}, pred[64]{0:T(512)(128)(4,1)S(1)}, u32[]{:S(2)}) copy-start(pred[64]{0:T(512)(128)(4,1)S(1)} %get-tuple-element.32) | copy-start | bytes 196
  15.5 8.6 %copy-start.20 = (pred[64]{0:T(512)(128)(4,1)}, pred[64]{0:T(512)(128)(4,1)S(1)}, u32[]{:S(2)}) copy-start(pred[64]{0:T(512)(128)(4,1)S(1)} %get-tuple-element.33) | copy-start | bytes 196
  78.4 1.5 copy-start.14
  78.4 1.6 copy-start.15
  81.6 5.3 %copy-start.1 = (f32[4,64,8,512]{3,2,1,0:T(8,128)}, f32[4,64,8,512]{3,2,1,0:T(8,128)S(1)}, u32[]{:S(2)}) copy-start(f32[4,64,8,512]{3,2,1,0:T(8,128)S(1)} %get-tuple-element.37) | copy-start | bytes 12582916
  82.5 4.4 %copy-start.3 = (f32[4,64,8,512]{3,2,1,0:T(8,128)}, f32[4,64,8,512]{3,2,1,0:T(8,128)S(1)}, u32[]{:S(2)}) copy-start(f32[4,64,8,512]{3,2,1,0:T(8,128)S(1)} %get-tuple-element.35) | copy-start | bytes 12582916
  83.3 1.3 copy-start.6
  84.6 2.3 %copy-start.19 = (pred[64]{0:T(512)(128)(4,1)S(1)}, pred[64]{0:T(512)(128)(4,1)}, u32[]{:S(2)}) copy-start(pred[64]{0:T(512)(128)(4,1)} %copy-done.18) | copy-start | bytes 196
  84.6 2.4 %copy-start.21 = (pred[64]{0:T(512)(128)(4,1)S(1)}, pred[64]{0:T(512)(128)(4,1)}, u32[]{:S(2)}) copy-start(pred[64]{0:T(512)(128)(4,1)} %copy-done.20) | copy-start | bytes 196
  84.6 2.5 %copy-start.4 = (bf16[2,1024,4,128]{3,2,1,0:T(4,128)(2,1)S(1)}, bf16[2,1024,4,128]{3,2,1,0:T(4,128)(2,1)}, u32[]{:S(2)}) copy-start(bf16[2,1024,4,128]{3,2,1,0:T(4,128)(2,1)} %reshape.290) | copy-start | bytes 6291460
  86.9 1.7 copy-start.25
  86.9 1.7 copy-start.26
  88.7 1.5 copy-start.12
  91.9 15.7 %all-to-all-start.1 = ((f32[8,1,256]{2,1,0:T(1,128)}), f32[8,1,256]{2,1,0:T(1,128)S(1)}, u32[]{:S(2)}, u32[]{:S(2)}) async-start(f32[8,1,256]{2,1,0:T(1,128)} %reshape.303), calls=%async_computation.1 | async-start | bytes 16384 | tf_op jit(solution)/shard_map/all_to_all | solution.py:181
  95.3 3.6 %copy-start.2 = (f32[4,64,8,512]{3,2,1,0:T(8,128)S(1)}, f32[4,64,8,512]{3,2,1,0:T(8,128)}, u32[]{:S(2)}) copy-start(f32[4,64,8,512]{3,2,1,0:T(8,128)} %copy-done.1) | copy-start | bytes 12582916
  95.3 3.7 %copy-start.8 = (bf16[1,512,512]{1,2,0:T(8,128)(2,1)S(1)}, bf16[1,512,512]{1,2,0:T(8,128)(2,1)}, u32[]{:S(2)}) copy-start(bf16[1,512,512]{1,2,0:T(8,128)(2,1)} %copy.243) | copy-start | bytes 1572868
  100.6 1.0 copy-start.5
  101.6 4.7 %copy-start.7 = (f32[2,8,4,8,8]{3,4,1,2,0:T(8,128)S(1)}, f32[2,8,4,8,8]{3,4,1,2,0:T(8,128)}, u32[]{:S(2)}) copy-start(f32[2,8,4,8,8]{3,4,1,2,0:T(8,128)} %copy-done.6) | copy-start | bytes 49156
  103.0 3.4 %copy-start.16 = (f32[2,8,4,8]{3,1,2,0:T(8,128)S(1)}, f32[2,8,4,8]{3,1,2,0:T(8,128)}, u32[]{:S(2)}) copy-start(f32[2,8,4,8]{3,1,2,0:T(8,128)} %get-tuple-element.24) | copy-start | bytes 6148
  103.0 3.7 %copy-start.13 = (f32[1,64,4,8]{3,1,2,0:T(8,128)S(1)}, f32[1,64,4,8]{3,1,2,0:T(8,128)}, u32[]{:S(2)}) copy-start(f32[1,64,4,8]{3,1,2,0:T(8,128)} %copy-done.12) | copy-start | bytes 24580
  107.6 10.5 %all-to-all-start.2 = ((f32[8,1,256]{2,1,0:T(1,128)}), f32[8,1,256]{2,1,0:T(1,128)S(1)}, u32[]{:S(2)}, u32[]{:S(2)}) async-start(f32[8,1,256]{2,1,0:T(1,128)} %reshape.305), calls=%async_computation.2 | async-start | bytes 16384 | tf_op jit(solution)/shard_map/all_to_all | solution.py:182
  118.0 30.1 %all-to-all-start = ((f32[1,64,4,8,128]{4,3,2,0,1:T(8,128)}), f32[1,64,4,8,128]{4,3,2,0,1:T(8,128)S(1)}, u32[]{:S(2)}, u32[]{:S(2)}) async-start(f32[1,64,4,8,128]{4,3,2,0,1:T(8,128)} %copy.197), calls=%async_computation | async-start | bytes 2097152 | tf_op jit(solution)/shard_map/all_to_all | solution.py:183
  121.6 58.1 %reduce-scatter.2.cloned.1.call-start = ((), (), s32[]{:S(2)}) async-start(), calls=%async_computation.4 | async-start | bytes 393216 | tf_op jit(solution)/shard_map/reduce_scatter | solution.py:192
Sparse Core Ops, SparseCore 0:
  14.9 63.4 all-reduce.2
  169.3 10.3 reduce-scatter.1
where the time goes:
time: 189 us; the launch traced here: 188 us
  waiting for transfers between devices  86.6 us (46%)
  local copies, waits for them, and re-layouts  26 us (14%)
  matrix products  24.8 us (13%)
  blocking collectives  14.9 us (8%)
  between operations  14 us (7%)
  starting transfers between devices  11.9 us (6%)
  other arithmetic  9.87 us (5%)
    psum x1, waiting for transfers between devices, body(): q_sum, k_sum, v_sum = lax.psum((q_part, k_part, v_part), ('roll', 'seq'))  49.9 us
    all_to_all x1, waiting for transfers between devices, body(): lax.all_to_all(numer_all[None], ('roll', 'seq'), split_axis=1, concat_axi...  23.6 us
    all_gather x1, blocking collectives, body(): attention = lax.all_gather(share, ('roll', 'seq'), axis=0, tiled=True)  14.9 us
    reduce_scatter x1, waiting for transfers between devices, body(): lax.psum_scatter(jnp.dot(attention, w_out, preferred_element_type=jnp.flo...  10.6 us
    unnamed x66, local copies, waits for them, and re-layouts  8.2 us
    dot_general x1, matrix products, body(): q_part = jnp.dot(hidden, w_query, preferred_element_type=jnp.float32)  6.18 us
    dot_general x1, matrix products, body(): jnp.dot(attention, w_out, preferred_element_type=jnp.float32)  5.67 us
    all_to_all x1, starting transfers between devices, body(): lax.all_to_all(total_all[None], ('roll', 'seq'), split_axis=1, concat_axi...  4.86 us
  transfers between devices with their start and end apart: 5, of which 4 were waited for; matrix products, arithmetic and copies ran while one was open for 16% of the time, Pallas kernels for 0%

commit v1 on v0

--- a/solution.py
+++ b/solution.py
@@ -71,6 +71,21 @@
     suffix_lengths,
     prompt_of,
 ):
+
+    def connect_islands(x_part, link_axis):
+        aux = jax.lax.axis_size(link_axis)
+        y1 = jax.lax.axis_index(link_axis)
+        later, carry_out = (aux, y1)
+        reply, v_next = (x_part, 1)
+        while v_next < later:
+            outer = tuple(((tick, tick ^ v_next) for tick in range(later)))
+            b_next = jax.lax.ppermute(reply, axis_name=link_axis, perm=outer)
+            formed = jnp.concatenate([reply, b_next], 0)
+            state_next = jnp.concatenate([b_next, reply], axis=0)
+            reply = jnp.where(carry_out & v_next == 0, formed, state_next)
+            v_next = 2 * v_next
+        return reply
+
     row_count = hidden.shape[0]
     q_heads = w_query.shape[1] // HD
     kv_heads = w_key.shape[1] // HD
@@ -188,7 +203,7 @@
         jnp.sum(numers * factors[..., None], axis=0) / jnp.sum(totals * factors, axis=0)[..., None]
     )
     share = share.astype(jnp.bfloat16).reshape(share.shape[0], q_heads * HD)
-    attention = lax.all_gather(share, ("roll", "seq"), axis=0, tiled=True)
+    attention = connect_islands(share, ("roll", "seq"))
     summed = lax.psum_scatter(
         jnp.dot(attention, w_out, preferred_element_type=jnp.float32),
         "tp",

time: 189 us -> 195 us (1.032)
  waiting for transfers between devices: 86.6 us -> 108 us
  blocking collectives: 14.9 us -> 0 us
    ppermute x0 -> x3, waiting for transfers between devices: none -> 20.7 us  [connect_islands(): b_next = jax.lax.ppermute(reply, axis_name=link_axis, perm=outer)]
    all_gather x1 -> x0, blocking collectives: 14.9 us -> none  [body(): attention = lax.all_gather(share, ('roll', 'seq'), axis=0, tiled=True)]
  transfers between devices with their start and end apart: 5 -> 8, of which waited for: 4 -> 7; matrix products, arithmetic and copies ran while one was open for 16% -> 15% of each run, Pallas kernels for 0% -> 0%
where the time goes in v1:
time: 195 us; the launch traced here: 194 us
  waiting for transfers between devices  108 us (55%)
  local copies, waits for them, and re-layouts  25.6 us (13%)
  matrix products  24.8 us (13%)
  between operations  14 us (7%)
  starting transfers between devices  12.2 us (6%)
  other arithmetic  9.96 us (5%)
    psum x1, waiting for transfers between devices, body(): q_sum, k_sum, v_sum = lax.psum((q_part, k_part, v_part), ('roll', 'seq'))  50 us
    all_to_all x1, waiting for transfers between devices, body(): lax.all_to_all(numer_all[None], ('roll', 'seq'), split_axis=1, concat_axi...  24 us
    ppermute x3, waiting for transfers between devices, connect_islands(): b_next = jax.lax.ppermute(reply, axis_name=link_axis, perm=outer)  20.7 us
    reduce_scatter x1, waiting for transfers between devices, body(): lax.psum_scatter(jnp.dot(attention, w_out, preferred_element_type=jnp.flo...  10.7 us
    unnamed x66, local copies, waits for them, and re-layouts  8.24 us
    dot_general x1, matrix products, body(): q_part = jnp.dot(hidden, w_query, preferred_element_type=jnp.float32)  6.16 us
    dot_general x1, matrix products, body(): jnp.dot(attention, w_out, preferred_element_type=jnp.float32)  5.66 us
    all_to_all x1, starting transfers between devices, body(): lax.all_to_all(total_all[None], ('roll', 'seq'), split_axis=1, concat_axi...  4.86 us
  transfers between devices with their start and end apart: 8, of which 7 were waited for; matrix products, arithmetic and copies ran while one was open for 15% of the time, Pallas kernels for 0%

profile of v1, /device:TPU:0, one launch (start us, length us, event | category | flops | bytes accessed | tf_op | source)
XLA Modules:
  0.0 194.5 jit_solution(2753239720130941171)
XLA Ops:
  6.6 6.2 %fusion.99 = f32[64,4096]{1,0:T(8,128)} fusion(bf16[64,1024]{1,0:T(8,128)(2,1)} %param.14, bf16[1024,4096]{1,0:T(8,128)(2,1)} %param.15), kind=kOutput, calls=%fused_computation.154 | convolution fusion | flops 536870912 | bytes 9568256 | tf_op jit(solution)/shard_map/dot_general | solution.py:99
  12.8 0.9 fusion.100
  13.8 1.0 fusion.101
  15.5 4.0 %reshape.290 = bf16[2,1024,4,128]{3,2,1,0:T(4,128)(2,1)} reshape(bf16[2,1024,512]{2,1,0:T(8,128)(2,1)} %param.24) | data formatting | bytes 4194304 | tf_op jit(solution)/shard_map/reshape | solution.py:151
  19.5 0.6 dynamic-slice.4
  20.0 0.7 dynamic-slice.5
  20.7 1.3 fusion.97
  22.0 1.0 copy.233
  23.0 1.0 copy.231
  24.0 4.0 %reshape.291 = bf16[2,1024,4,128]{3,2,1,0:T(4,128)(2,1)} reshape(bf16[2,1024,512]{2,1,0:T(8,128)(2,1)} %param.25) | data formatting | bytes 4194304 | tf_op jit(solution)/shard_map/reshape | solution.py:152
  28.4 50.0 %all-reduce.3.cloned.1.call-done = (f32[64,4096]{1,0:T(8,128)}, f32[64,512]{1,0:T(8,128)}, f32[64,512]{1,0:T(8,128)}) async-done(((f32[64,4096]{1,0:T(8,128)}, f32[64,512]{1,0:T(8,128)}, f32[64,512]{1,0:T(8,128)}), (f32[64,4096]{1,0:T(8,128)}, f32[64,512]{1,0:T(8,128)}, f32[64,512]{1,0:T(8,128)})) %all-reduce.3.cloned.1.call-update) | async-done | bytes 1310736 | tf_op jit(solution)/shard_map/psum | solution.py:102
  78.4 1.3 add_bitcast_fusion
  80.1 0.5 fusion.50
  80.7 0.9 bitcast_reduce_fusion.1
  81.6 0.9 bitcast_reduce_fusion
  82.5 0.7 select_reduce_fusion
  83.5 1.1 copy-done.6
  84.6 2.3 %fusion.2 = (f32[64,4,8]{2,0,1:T(8,128)S(1)}, f32[64,4,8]{2,0,1:T(8,128)S(1)}) fusion(f32[4,64,8,512]{3,2,1,0:T(8,128)S(1)} %get-tuple-element.37, f32[64,4,8]{2,0,1:T(8,128)S(1)} %get-tuple-element.36, f32[64,4,8]{2,0,1:T(8,128)S(1)} %get-tuple-element.34, f32[4,64,8,512]{3,2,1,0:T(8,128)S(1)} %get-tuple-element.35), kind=kLoop, calls=%fused_computation.6 | loop fusion | flops 6287360 | bytes 8421376 | tf_op jit(solution)/shard_map/reduce_sum | solution.py:140
  87.1 0.9 fusion.12
  88.0 0.6 fusion.21
  88.7 0.7 fusion.70
  89.4 0.7 copy.312
  90.2 1.7 reshape.303
  91.8 3.4 %all-to-all-start.1 = ((f32[8,1,256]{2,1,0:T(1,128)}), f32[8,1,256]{2,1,0:T(1,128)S(1)}, u32[]{:S(2)}, u32[]{:S(2)}) async-start(f32[8,1,256]{2,1,0:T(1,128)} %reshape.303), calls=%async_computation.1 | async-start | bytes 16384 | tf_op jit(solution)/shard_map/all_to_all | solution.py:196
  95.3 3.2 %fusion.26 = f32[4,64,8,128]{3,2,1,0:T(8,128)S(1)} fusion(bf16[512,4,128,1]{0,2,3,1:T(8,128)(2,1)} %bitcast.188, f32[4,64,8,512]{3,2,1,0:T(8,128)} %copy-done.3, f32[64,4,8]{2,0,1:T(8,128)S(1)} %get-tuple-element.34, pred[64]{0:T(512)(128)(4,1)} %copy-done.20), kind=kOutput, calls=%fused_computation.28 | convolution fusion | flops 271843328 | bytes 5775424 | tf_op jit(solution)/shard_map/tkgs,skd->tkgd/dot_general | solution.py:132
  98.5 0.4 copy-done.2
  99.0 1.6 fusion.23
  100.6 1.0 copy-done.5
  101.6 0.7 constant_dynamic-slice_fusion.2
  102.3 0.6 convert_element_type.64
  103.0 0.8 constant_dynamic-slice_fusion
  103.7 2.6 %fusion.41 = f32[2,8,4,8,128]{4,3,1,2,0:T(8,128)S(1)} fusion(bf16[2,1024,4,128,1]{3,2,1,0,4:T(4,128)(2,1)} %bitcast.191, f32[2,4,8,8,1024]{4,3,2,1,0:T(8,128)S(1)} %get-tuple-element.39, f32[2,8,4,8]{3,1,2,0:T(8,128)S(1)} %get-tuple-element.38, pred[2,1024]{1,0:T(4,128)(4,1)S(1)} %iota_compare_fusion, f32[2,8,4,8,128]{4,3,1,0,2:T(8,128)} %bitcast.201, ...), kind=kOutput, calls=%fused_computation.37 | convolution fusion | flops 136577024 | bytes 4728832 | tf_op jit(solution)/shard_map/rtkgs,rskd->rtkgd/dot_general | solution.py:49
  106.8 0.8 reshape.305
  107.6 4.9 %all-to-all-start.2 = ((f32[8,1,256]{2,1,0:T(1,128)}), f32[8,1,256]{2,1,0:T(1,128)S(1)}, u32[]{:S(2)}, u32[]{:S(2)}) async-start(f32[8,1,256]{2,1,0:T(1,128)} %reshape.305), calls=%async_computation.2 | async-start | bytes 16384 | tf_op jit(solution)/shard_map/all_to_all | solution.py:197
  112.4 0.7 constant_dynamic-update-slice_fusion
  113.2 2.4 %copy.188 = f32[1,64,4,8,128]{4,3,2,0,1:T(8,128)} copy(f32[1,64,4,8,128]{4,3,1,2,0:T(8,128)} %constant_dynamic-update-slice_fusion) | data formatting | bytes 2097152 | tf_op jit(solution)/shard_map/dynamic_update_slice | solution.py:192
  115.5 2.5 %all-to-all-done.2 = f32[8,1,256]{2,1,0:T(1,128)S(1)} async-done(((f32[8,1,256]{2,1,0:T(1,128)}), f32[8,1,256]{2,1,0:T(1,128)S(1)}, u32[]{:S(2)}, u32[]{:S(2)}) %all-to-all-start.2) | async-done | bytes 8224 | tf_op jit(solution)/shard_map/all_to_all | solution.py:197
  118.0 3.6 %all-to-all-start = ((f32[1,64,4,8,128]{4,3,2,0,1:T(8,128)}), f32[1,64,4,8,128]{4,3,2,0,1:T(8,128)S(1)}, u32[]{:S(2)}, u32[]{:S(2)}) async-start(f32[1,64,4,8,128]{4,3,2,0,1:T(8,128)} %copy.188), calls=%async_computation | async-start | bytes 2097152 | tf_op jit(solution)/shard_map/all_to_all | solution.py:198
  121.7 0.5 broadcast.227
  122.2 0.7 reduce.1
  123.0 0.7 reduce
  124.1 24.0 %all-to-all-done = f32[1,64,4,8,128]{4,3,2,0,1:T(8,128)S(1)} async-done(((f32[1,64,4,8,128]{4,3,2,0,1:T(8,128)}), f32[1,64,4,8,128]{4,3,2,0,1:T(8,128)S(1)}, u32[]{:S(2)}, u32[]{:S(2)}) %all-to-all-start) | async-done | bytes 1048608 | tf_op jit(solution)/shard_map/all_to_all | solution.py:198
  148.7 1.2 collective-permute-done
  150.0 5.5 %collective-permute-done.1 = bf16[16,4096]{1,0:T(8,128)(2,1)S(1)} collective-permute-done((bf16[16,4096]{1,0:T(8,128)(2,1)S(1)}, bf16[16,4096]{1,0:T(8,128)(2,1)S(1)}, u32[]{:S(2)}, u32[]{:S(2)}) %collective-permute-start.1) | collective-permute-done | bytes 131104 | tf_op jit(solution)/shard_map/ppermute | solution.py:82
  155.8 13.9 %collective-permute-done.2 = bf16[32,4096]{1,0:T(8,128)(2,1)S(1)} collective-permute-done((bf16[32,4096]{1,0:T(8,128)(2,1)S(1)}, bf16[32,4096]{1,0:T(8,128)(2,1)S(1)}, u32[]{:S(2)}, u32[]{:S(2)}) %collective-permute-start.2) | collective-permute-done | bytes 262176 | tf_op jit(solution)/shard_map/ppermute | solution.py:82
  169.7 5.7 %fusion.52 = f32[64,1024]{1,0:T(8,128)} fusion(bf16[4096,1024]{1,0:T(8,128)(2,1)} %param.21, bf16[32,4096]{1,0:T(8,128)(2,1)S(1)} %collective-permute-done.2, bf16[32,4096]{1,0:T(8,128)(2,1)S(1)} %maximum_select_fusion.2, pred[]{:T(512)S(6)} %eq.64), kind=kOutput, calls=%fused_computation.51 | convolution fusion | flops 539230208 | bytes 9175041 | tf_op jit(solution)/shard_map/dot_general | solution.py:208
  175.4 10.7 %reduce-scatter.2.cloned.1.call-done = f32[32,1024]{1,0:T(8,128)} async-done(((f32[64,1024]{1,0:T(8,128)}), f32[32,1024]{1,0:T(8,128)}) %reduce-scatter.2.cloned.1.call-update) | async-done | bytes 131088 | tf_op jit(solution)/shard_map/reduce_scatter | solution.py:207
  186.1 1.5 convert_element_type.68
  (100 shorter events, 4.0 us)
Async XLA Ops:
  6.5 6.2 %copy-start = (bf16[1024,512]{1,0:T(8,128)(2,1)S(1)}, bf16[1024,512]{1,0:T(8,128)(2,1)}, u32[]{:S(2)}) copy-start(bf16[1024,512]{1,0:T(8,128)(2,1)} %param.16) | copy-start | bytes 3145732
  6.5 6.2 %copy-start.9 = (bf16[64,1024]{1,0:T(8,128)(2,1)S(1)}, bf16[64,1024]{1,0:T(8,128)(2,1)}, u32[]{:S(2)}) copy-start(bf16[64,1024]{1,0:T(8,128)(2,1)} %param.14) | copy-start | bytes 393220
  6.5 7.2 %copy-start.10 = (bf16[1024,512]{1,0:T(8,128)(2,1)S(1)}, bf16[1024,512]{1,0:T(8,128)(2,1)}, u32[]{:S(2)}) copy-start(bf16[1024,512]{1,0:T(8,128)(2,1)} %param.17) | copy-start | bytes 3145732
  6.5 8.2 %copy-start.17 = (bf16[4096]{0:T(1024)(128)(2,1)S(1)}, bf16[4096]{0:T(1024)(128)(2,1)}, u32[]{:S(2)}) copy-start(bf16[4096]{0:T(1024)(128)(2,1)} %param.18) | copy-start | bytes 24580
  6.5 8.2 %copy-start.23 = (bf16[512]{0:T(512)(128)(2,1)S(1)}, bf16[512]{0:T(512)(128)(2,1)}, u32[]{:S(2)}) copy-start(bf16[512]{0:T(512)(128)(2,1)} %param.19) | copy-start | bytes 3076
  6.5 8.3 %copy-start.24 = (bf16[512]{0:T(512)(128)(2,1)S(1)}, bf16[512]{0:T(512)(128)(2,1)}, u32[]{:S(2)}) copy-start(bf16[512]{0:T(512)(128)(2,1)} %param.20) | copy-start | bytes 3076
  6.6 71.8 %all-reduce.3.cloned.1.call-start = ((), (), s32[]{:S(2)}) async-start(), calls=%async_computation.5 | async-start | bytes 2621440 | tf_op jit(solution)/shard_map/psum | solution.py:102
  12.8 2.1 %copy-start.11 = (bf16[2,512,512]{2,1,0:T(8,128)(2,1)S(1)}, bf16[2,512,512]{2,1,0:T(8,128)(2,1)}, u32[]{:S(2)}) copy-start(bf16[2,512,512]{2,1,0:T(8,128)(2,1)} %param.22) | copy-start | bytes 3145732
  12.8 2.6 %copy-start.22 = (s32[8]{0:T(128)S(1)}, s32[8]{0:T(128)}, u32[]{:S(2)}) copy-start(s32[8]{0:T(128)} %param.26) | copy-start | bytes 100
  12.8 2.6 %copy-start.27 = (s32[8]{0:T(128)S(1)}, s32[8]{0:T(128)}, u32[]{:S(2)}) copy-start(s32[8]{0:T(128)} %param.27) | copy-start | bytes 100
  15.5 8.6 %copy-start.18 = (pred[64]{0:T(512)(128)(4,1)}, pred[64]{0:T(512)(128)(4,1)S(1)}, u32[]{:S(2)}) copy-start(pred[64]{0:T(512)(128)(4,1)S(1)} %get-tuple-element.32) | copy-start | bytes 196
  15.5 8.5 %copy-start.20 = (pred[64]{0:T(512)(128)(4,1)}, pred[64]{0:T(512)(128)(4,1)S(1)}, u32[]{:S(2)}) copy-start(pred[64]{0:T(512)(128)(4,1)S(1)} %get-tuple-element.33) | copy-start | bytes 196
  78.4 1.5 copy-start.14
  78.4 1.6 copy-start.15
  81.6 5.3 %copy-start.1 = (f32[4,64,8,512]{3,2,1,0:T(8,128)}, f32[4,64,8,512]{3,2,1,0:T(8,128)S(1)}, u32[]{:S(2)}) copy-start(f32[4,64,8,512]{3,2,1,0:T(8,128)S(1)} %get-tuple-element.37) | copy-start | bytes 12582916
  82.5 4.4 %copy-start.3 = (f32[4,64,8,512]{3,2,1,0:T(8,128)}, f32[4,64,8,512]{3,2,1,0:T(8,128)S(1)}, u32[]{:S(2)}) copy-start(f32[4,64,8,512]{3,2,1,0:T(8,128)S(1)} %get-tuple-element.35) | copy-start | bytes 12582916
  83.3 1.3 copy-start.6
  84.6 2.3 %copy-start.19 = (pred[64]{0:T(512)(128)(4,1)S(1)}, pred[64]{0:T(512)(128)(4,1)}, u32[]{:S(2)}) copy-start(pred[64]{0:T(512)(128)(4,1)} %copy-done.18) | copy-start | bytes 196
  84.6 2.4 %copy-start.21 = (pred[64]{0:T(512)(128)(4,1)S(1)}, pred[64]{0:T(512)(128)(4,1)}, u32[]{:S(2)}) copy-start(pred[64]{0:T(512)(128)(4,1)} %copy-done.20) | copy-start | bytes 196
  84.6 2.5 %copy-start.4 = (bf16[2,1024,4,128]{3,2,1,0:T(4,128)(2,1)S(1)}, bf16[2,1024,4,128]{3,2,1,0:T(4,128)(2,1)}, u32[]{:S(2)}) copy-start(bf16[2,1024,4,128]{3,2,1,0:T(4,128)(2,1)} %reshape.290) | copy-start | bytes 6291460
  86.9 1.7 copy-start.25
  86.9 1.7 copy-start.26
  88.7 1.5 copy-start.12
  91.8 15.7 %all-to-all-start.1 = ((f32[8,1,256]{2,1,0:T(1,128)}), f32[8,1,256]{2,1,0:T(1,128)S(1)}, u32[]{:S(2)}, u32[]{:S(2)}) async-start(f32[8,1,256]{2,1,0:T(1,128)} %reshape.303), calls=%async_computation.1 | async-start | bytes 16384 | tf_op jit(solution)/shard_map/all_to_all | solution.py:196
  95.3 3.6 %copy-start.2 = (f32[4,64,8,512]{3,2,1,0:T(8,128)S(1)}, f32[4,64,8,512]{3,2,1,0:T(8,128)}, u32[]{:S(2)}) copy-start(f32[4,64,8,512]{3,2,1,0:T(8,128)} %copy-done.1) | copy-start | bytes 12582916
  95.3 3.7 %copy-start.8 = (bf16[1,512,512]{1,2,0:T(8,128)(2,1)S(1)}, bf16[1,512,512]{1,2,0:T(8,128)(2,1)}, u32[]{:S(2)}) copy-start(bf16[1,512,512]{1,2,0:T(8,128)(2,1)} %copy.231) | copy-start | bytes 1572868
  100.6 1.0 copy-start.5
  101.6 4.8 %copy-start.7 = (f32[2,8,4,8,8]{3,4,1,2,0:T(8,128)S(1)}, f32[2,8,4,8,8]{3,4,1,2,0:T(8,128)}, u32[]{:S(2)}) copy-start(f32[2,8,4,8,8]{3,4,1,2,0:T(8,128)} %copy-done.6) | copy-start | bytes 49156
  103.0 3.4 %copy-start.16 = (f32[2,8,4,8]{3,1,2,0:T(8,128)S(1)}, f32[2,8,4,8]{3,1,2,0:T(8,128)}, u32[]{:S(2)}) copy-start(f32[2,8,4,8]{3,1,2,0:T(8,128)} %get-tuple-element.24) | copy-start | bytes 6148
  103.0 3.7 %copy-start.13 = (f32[1,64,4,8]{3,1,2,0:T(8,128)S(1)}, f32[1,64,4,8]{3,1,2,0:T(8,128)}, u32[]{:S(2)}) copy-start(f32[1,64,4,8]{3,1,2,0:T(8,128)} %copy-done.12) | copy-start | bytes 24580
  107.6 10.5 %all-to-all-start.2 = ((f32[8,1,256]{2,1,0:T(1,128)}), f32[8,1,256]{2,1,0:T(1,128)S(1)}, u32[]{:S(2)}, u32[]{:S(2)}) async-start(f32[8,1,256]{2,1,0:T(1,128)} %reshape.305), calls=%async_computation.2 | async-start | bytes 16384 | tf_op jit(solution)/shard_map/all_to_all | solution.py:197
  118.0 30.1 %all-to-all-start = ((f32[1,64,4,8,128]{4,3,2,0,1:T(8,128)}), f32[1,64,4,8,128]{4,3,2,0,1:T(8,128)S(1)}, u32[]{:S(2)}, u32[]{:S(2)}) async-start(f32[1,64,4,8,128]{4,3,2,0,1:T(8,128)} %copy.188), calls=%async_computation | async-start | bytes 2097152 | tf_op jit(solution)/shard_map/all_to_all | solution.py:198
  121.6 64.5 %reduce-scatter.2.cloned.1.call-start = ((), (), s32[]{:S(2)}) async-start(), calls=%async_computation.4 | async-start | bytes 393216 | tf_op jit(solution)/shard_map/reduce_scatter | solution.py:207
  148.6 1.3 collective-permute-start
  149.9 5.6 %collective-permute-start.1 = (bf16[16,4096]{1,0:T(8,128)(2,1)S(1)}, bf16[16,4096]{1,0:T(8,128)(2,1)S(1)}, u32[]{:S(2)}, u32[]{:S(2)}) collective-permute-start(bf16[16,4096]{1,0:T(8,128)(2,1)S(1)} %maximum_select_fusion.3), channel_id=1, source_target_pairs={{0,4},{1,5},{4,0},{5,1},{8,12},{9,13},{12,8},{13,9},{2,6},{3,7},{6... | collective-permute-start | bytes 393224 | tf_op jit(solution)/shard_map/ppermute | solution.py:82
  155.6 14.1 %collective-permute-start.2 = (bf16[32,4096]{1,0:T(8,128)(2,1)S(1)}, bf16[32,4096]{1,0:T(8,128)(2,1)S(1)}, u32[]{:S(2)}, u32[]{:S(2)}) collective-permute-start(bf16[32,4096]{1,0:T(8,128)(2,1)S(1)} %maximum_select_fusion.2), channel_id=1, source_target_pairs={{0,8},{1,9},{4,12},{5,13},{8,0},{9,1},{12,4},{13,5},{2,10},{3,11},... | collective-permute-start | bytes 786440 | tf_op jit(solution)/shard_map/ppermute | solution.py:82
Sparse Core Ops, SparseCore 0:
  14.9 63.4 all-reduce.2
  175.5 10.5 reduce-scatter.1
